TPU v7x, 32 devices: a whole 2x2x4 slice. The times are simulated.
32 devices in a mesh: stream: 4 (over z), cross: 4 (over y, x), pair: 2 (over core).
Axes of the slice: x: 2, y: 2, z: 4, core: 2. Of those that a mesh axis runs over, the one named last changes fastest.
Arguments:
- krylov_basis: float32 [4, 4, 4, 64, 320], P(None, None, 'stream', ('cross', 'pair')), may hold values from -6 to 6
- inverse_blocks: bfloat16 [4, 64, 320, 320], P('stream', ('cross', 'pair'))
- inflow_lift: bfloat16 [4, 64, 320, 80], P('stream', ('cross', 'pair')), may hold values from -0.625 to 0.625
- outflow_trace: bfloat16 [4, 64, 80, 320], P('stream', ('cross', 'pair')), may hold values from -0.3125 to 0.3125
- cross_lift: bfloat16 [4, 64, 320, 80], P('stream', ('cross', 'pair')), may hold values from -0.625 to 0.625
- cross_trace: bfloat16 [4, 64, 80, 320], P('stream', ('cross', 'pair')), may hold values from -0.3125 to 0.3125
- upwind_element: int32 [4, 64], P('stream', ('cross', 'pair')), may hold values from 0 to 7
- cross_element: int32 [4, 64], P('stream', ('cross', 'pair')), may hold values from 0 to 63
Outputs:
- next_vector: float32 [4, 4, 64, 320], P(None, 'stream', ('cross', 'pair'))
- hessenberg: float32 [5, 4], replicated
Inputs may be any that keep to these rules, and one draw needn't show every extreme that they name: upwind_element names one of the 8 elements held by the device one partition upstream at the same cross-stream place; at streamwise position 0 it is not read. cross_element names any element at the same streamwise position.
All inputs are finite; a program needn't handle non-finite values.
Results may differ from a plain program's by a relative error of at most 0.0003.
Values sent between devices are 32-bit elements; how exact they have to be, the bound alone decides.
A program may use at most 64 MiB of HBM per device.

v0:
```python
import jax
import jax.numpy as jnp
from jax import lax
from jax.sharding import PartitionSpec as P

E = 8
B = 320
R = 80
NV = 4
KB = 4


highest = lax.Precision.HIGHEST


def carried_in(part, axis, combine, identity):
    place = lax.axis_index(axis)
    gathered = jax.tree.map(lambda a: lax.all_gather(a, axis), part)
    state = jax.tree.map(lambda a, e: jnp.zeros_like(a) + jnp.asarray(e, a.dtype), part, identity)

    def one(hop, state):
        return combine(
            state, jax.tree.map(lambda a: lax.dynamic_index_in_dim(a, hop, 0, False), gathered)
        )

    return lax.fori_loop(0, place, one, state)


def compose(earlier, following):
    first_gain, first_hot, first_offset = earlier
    second_gain, second_hot, second_offset = following
    picked_gain = jnp.einsum("ek,krs->ers", second_hot, first_gain, precision=highest)
    joined_gain = jnp.einsum("ers,est->ert", second_gain, picked_gain, precision=highest)
    joined_hot = jnp.dot(second_hot, first_hot, precision=highest)
    picked_offset = jnp.einsum("ek,nkr->ner", second_hot, first_offset, precision=highest)
    joined_offset = second_offset + jnp.einsum(
        "ers,nes->ner", second_gain, picked_offset, precision=highest
    )
    return (joined_gain, joined_hot, joined_offset)


def local(
    krylov_basis,
    inverse_blocks,
    inflow_lift,
    outflow_trace,
    cross_lift,
    cross_trace,
    upwind_element,
    cross_element,
):
    basis_local = krylov_basis[:, :, 0]
    current = basis_local[KB - 1]
    inverse_local = inverse_blocks[0].astype(jnp.float32)
    lift_local = inflow_lift[0].astype(jnp.float32)
    trace_local = outflow_trace[0].astype(jnp.float32)
    upwind_onehot = (upwind_element[0][:, None] == jnp.arange(E, dtype=jnp.int32)[None, :]).astype(
        jnp.float32
    )
    traced_inverse = jnp.einsum("erb,ebc->erc", trace_local, inverse_local, precision=highest)
    step_gain = -jnp.einsum("erc,ecs->ers", traced_inverse, lift_local, precision=highest)
    offset_faces = jnp.einsum("erc,nec->ner", traced_inverse, current, precision=highest)
    identity = (
        jnp.broadcast_to(jnp.eye(R, dtype=jnp.float32), (E, R, R)),
        jnp.eye(E, dtype=jnp.float32),
        jnp.zeros((NV, E, R), jnp.float32),
    )
    prefix = carried_in((step_gain, upwind_onehot, offset_faces), "stream", compose, identity)
    previous = prefix[2]
    inflow = jnp.einsum("ek,nkr->ner", upwind_onehot, previous, precision=highest)
    right_side = current - jnp.einsum("ebr,ner->neb", lift_local, inflow, precision=highest)
    relaxed = jnp.einsum("ebc,nec->neb", inverse_local, right_side, precision=highest)
    face_data = jnp.einsum(
        "erb,neb->ner", cross_trace[0].astype(jnp.float32), relaxed, precision=highest
    )
    gathered = lax.all_gather(face_data, ("cross", "pair"), axis=1, tiled=True)
    group_width = gathered.shape[1]
    cross_onehot = (
        cross_element[0][:, None] == jnp.arange(group_width, dtype=jnp.int32)[None, :]
    ).astype(jnp.float32)
    read_faces = jnp.einsum("eg,ngr->ner", cross_onehot, gathered, precision=highest)
    image = current + jnp.einsum(
        "ebr,ner->neb", cross_lift[0].astype(jnp.float32), read_faces, precision=highest
    )
    total_dofs = float(
        E * B * lax.axis_size("stream") * lax.axis_size("cross") * lax.axis_size("pair")
    )
    projections = jnp.einsum("kneb,neb->kn", basis_local, image, precision=highest)
    coeffs = lax.psum(projections, ("stream", "cross", "pair")) / total_dofs
    orthogonal = image - jnp.einsum("kn,kneb->neb", coeffs, basis_local, precision=highest)
    squares = lax.psum(jnp.sum(orthogonal * orthogonal, axis=(1, 2)), ("stream", "cross", "pair"))
    new_norm = jnp.sqrt(squares / total_dofs + 1e-06)
    next_vector = (orthogonal / new_norm[:, None, None])[:, None]
    return (next_vector, jnp.concatenate([coeffs, new_norm[None, :]], axis=0))


def solution(mesh):
    return jax.shard_map(
        local,
        mesh=mesh,
        in_specs=(
            P(None, None, "stream", ("cross", "pair"), None),
            P("stream", ("cross", "pair"), None, None),
            P("stream", ("cross", "pair"), None, None),
            P("stream", ("cross", "pair"), None, None),
            P("stream", ("cross", "pair"), None, None),
            P("stream", ("cross", "pair"), None, None),
            P("stream", ("cross", "pair")),
            P("stream", ("cross", "pair")),
        ),
        out_specs=(P(None, "stream", ("cross", "pair"), None), P()),
        check_vma=False,
    )
```

profile of v0, /device:TPU:0, one launch (start us, length us, event | category | flops | bytes accessed | tf_op | source)
XLA Modules:
  0.0 156.7 jit_solution(11396231571596374050)
XLA Ops:
  0.6 0.0 copy-start
  0.6 0.9 slice.4
  1.6 0.6 copy-done
  2.2 0.0 copy-start.1
  2.2 1.6 %fusion.13 = f32[8,80,320]{2,1,0:T(8,128)S(1)} fusion(bf16[1,8,320,320]{3,2,1,0:T(8,128)(2,1)S(1)} %copy-done, bf16[1,8,80,320]{3,2,1,0:T(8,128)(2,1)} %param.13), kind=kOutput, calls=%fused_computation.16 | convolution fusion | flops 131072000 | bytes 2867200 | tf_op jit(solution)/shard_map/erb,ebc->erc/dot_general | solution.py:60
  3.8 1.2 convolution_bitcast_fusion.4
  5.0 0.0 copy-start.5
  5.0 15.1 %all-gather = f32[16,8,80]{2,1,0:T(8,128)S(1)} all-gather(f32[4,8,80]{2,1,0:T(8,128)S(1)} %copy.15), channel_id=2, replica_groups=mesh['stream'=4,'cross'=4,'pair'=2] {'stream'}, dimensions={0}, use_global_device_ids=true | all-gather | bytes 51200 | tf_op jit(solution)/shard_map/all_gather | solution.py:18
  20.1 0.0 copy-done.1
  20.1 0.7 convolution_negate_fusion
  20.8 24.8 %all-gather.1 = f32[32,80,80]{2,1,0:T(8,128)S(1)} all-gather(f32[8,80,80]{2,1,0:T(8,128)S(1)} %convolution_negate_fusion), channel_id=3, replica_groups=mesh['stream'=4,'cross'=4,'pair'=2] {'stream'}, dimensions={0}, use_global_device_ids=true | all-gather | bytes 1024000 | tf_op jit(solution)/shard_map/all_gather | solution.py:18
  45.6 0.0 copy-done.5
  45.6 0.1 fusion.35
  45.6 13.2 %all_gather.21 = f32[4,8,8]{2,1,0:T(8,128)S(1)} all-gather(f32[1,8,8]{2,1,0:T(8,128)S(1)} %fusion.35), channel_id=1, replica_groups=mesh['stream'=4,'cross'=4,'pair'=2] {'stream'}, dimensions={0}, use_global_device_ids=true | all-gather | bytes 1280 | tf_op jit(solution)/shard_map/all_gather | solution.py:18
  58.8 0.0 copy-start.2
  58.9 0.0 copy-start.6
  58.9 0.0 copy-start.3
  58.9 0.3 convolution_bitcast_fusion.1
  59.2 0.1 copy.22
  59.3 0.0 copy-start.4
  59.3 1.5 fusion.19
  60.7 1.7 %fusion.15 = f32[4,8,320]{2,0,1:T(4,128)S(1)} fusion(f32[4,8,320]{2,0,1:T(4,128)S(1)} %fusion.19, bf16[1,8,320,320]{3,2,1,0:T(8,128)(2,1)S(1)} %copy-done), kind=kOutput, calls=%fused_computation.20 | convolution fusion | flops 39321600 | bytes 1720320 | tf_op jit(solution)/shard_map/ebc,nec->neb/dot_general | solution.py:72
  62.5 0.0 copy-done.2
  62.5 0.6 convolution_bitcast_fusion.5
  63.1 9.2 %all_gather.24 = f32[4,64,80]{2,0,1:T(4,128)S(1)} all-gather(f32[4,8,80]{2,0,1:T(4,128)S(1)} %convolution_bitcast_fusion.5), channel_id=1, replica_groups=mesh['stream'=4,'cross'=4,'pair'=2] {'cross','pair'}, dimensions={1}, use_global_device_ids=true | all-gather | bytes 92160 | tf_op jit(solution)/shard_map/all_gather | solution.py:76
  72.3 0.0 copy-done.6
  72.3 0.2 fusion.29
  72.5 0.0 copy-done.3
  72.5 0.4 fusion.18
  72.9 0.0 copy-done.4
  72.9 1.0 fusion.27
  73.8 39.1 %psum.14 = f32[4,4]{0,1:T(4,128)S(1)} all-reduce(f32[4,4]{0,1:T(4,128)S(1)} %bitcast.119), channel_id=1, replica_groups=mesh['stream'=4,'cross'=4,'pair'=2] {'stream','cross','pair'}, use_global_device_ids=true, to_apply=%region_2.3 | all-reduce | flops 16 | bytes 128 | tf_op jit(solution)/shard_map/psum | solution.py:89
  113.0 0.5 fusion.25
  113.5 0.1 multiply_reduce_fusion
  113.7 41.5 %psum.15 = f32[4]{0:T(128)S(1)} all-reduce(f32[4]{0:T(128)S(1)} %multiply_reduce_fusion), channel_id=1, replica_groups=mesh['stream'=4,'cross'=4,'pair'=2] {'stream','cross','pair'}, use_global_device_ids=true, to_apply=%region_4.5 | all-reduce | flops 4 | bytes 32 | tf_op jit(solution)/shard_map/psum | solution.py:91
  155.2 0.1 divide_bitcast_fusion
  155.3 0.6 copy.18
  155.9 0.1 copy.17
  156.0 0.7 pad_maximum_fusion
  (5 shorter events, 0.0 us)
Async XLA Ops:
  0.6 1.6 %copy-start = (bf16[1,8,320,320]{3,2,1,0:T(8,128)(2,1)S(1)}, bf16[1,8,320,320]{3,2,1,0:T(8,128)(2,1)}, u32[]{:S(2)}) copy-start(bf16[1,8,320,320]{3,2,1,0:T(8,128)(2,1)} %param.11) | copy-start | bytes 4915204
  2.2 17.9 %copy-start.1 = (bf16[1,8,320,80]{2,3,1,0:T(8,128)(2,1)S(1)}, bf16[1,8,320,80]{2,3,1,0:T(8,128)(2,1)}, u32[]{:S(2)}) copy-start(bf16[1,8,320,80]{2,3,1,0:T(8,128)(2,1)} %param.12) | copy-start | bytes 1228804
  5.0 40.6 %copy-start.5 = (s32[1,8]{1,0:T(1,128)S(1)}, s32[1,8]{1,0:T(1,128)}, u32[]{:S(2)}) copy-start(s32[1,8]{1,0:T(1,128)} %param.16) | copy-start | bytes 100
  58.8 3.6 %copy-start.2 = (bf16[1,8,80,320]{3,2,1,0:T(8,128)(2,1)S(1)}, bf16[1,8,80,320]{3,2,1,0:T(8,128)(2,1)}, u32[]{:S(2)}) copy-start(bf16[1,8,80,320]{3,2,1,0:T(8,128)(2,1)} %param.15) | copy-start | bytes 1228804
  58.9 13.5 %copy-start.6 = (s32[1,8]{1,0:T(1,128)S(1)}, s32[1,8]{1,0:T(1,128)}, u32[]{:S(2)}) copy-start(s32[1,8]{1,0:T(1,128)} %param.17) | copy-start | bytes 100
  58.9 13.6 %copy-start.3 = (bf16[1,8,320,80]{2,3,1,0:T(8,128)(2,1)S(1)}, bf16[1,8,320,80]{2,3,1,0:T(8,128)(2,1)}, u32[]{:S(2)}) copy-start(bf16[1,8,320,80]{2,3,1,0:T(8,128)(2,1)} %param.14) | copy-start | bytes 1228804
  59.3 13.6 %copy-start.4 = (f32[4,4,1,8,320]{4,3,2,1,0:T(8,128)S(1)}, f32[4,4,1,8,320]{4,3,2,1,0:T(8,128)}, u32[]{:S(2)}) copy-start(f32[4,4,1,8,320]{4,3,2,1,0:T(8,128)} %param.10) | copy-start | bytes 491524
where the time goes:
time: 157 us
  blocking collectives  143 us (91%)
  matrix products  9.66 us (6%)
  local copies, waits for them, and re-layouts  2.4 us (2%)
    all_gather x3, blocking collectives, carried_in(): gathered = jax.tree.map(lambda a: lax.all_gather(a, axis), part)  53.1 us
    psum x1, blocking collectives, local(): lax.psum(jnp.sum(orthogonal * orthogonal, axis=(1, 2)), ('stream', 'cross...  41.5 us
    psum x1, blocking collectives, local(): coeffs = lax.psum(projections, ('stream', 'cross', 'pair')) / total_dofs  39.1 us
    all_gather x1, blocking collectives, local(): gathered = lax.all_gather(face_data, ('cross', 'pair'), axis=1, tiled=True)  9.22 us

commit v1 on v0

v1 whole, which is shorter than its diff:
```python
import functools

import jax
import jax.numpy as jnp
from jax import lax
from jax.experimental import pallas as pl
from jax.experimental.pallas import tpu as pltpu
from jax.sharding import PartitionSpec as P

E = 8
B = 320
R = 80
NV = 4
KB = 4
MESH = pl.DeviceIdType.MESH
GRAM = [(k, l) for k in range(KB) for l in range(k, KB)]
STATS = KB + 1 + len(GRAM)
ROWS = 64
GROUP = 2


def split(x):
    hi = x.astype(jnp.bfloat16)
    return hi, (x - hi.astype(jnp.float32)).astype(jnp.bfloat16)


def dot(a, b):
    return jnp.dot(a, b, preferred_element_type=jnp.float32)


def dot_t(a, b):
    return lax.dot_general(a, b, (((1,), (1,)), ((), ())), preferred_element_type=jnp.float32)


def two_rows(x):
    hi = x.astype(jnp.bfloat16).astype(jnp.float32)
    return jnp.concatenate([hi, x - hi], axis=0).astype(jnp.bfloat16)


def fold(x):
    return x[:NV] + x[NV:]


def kernel(
    sizes,
    kry_hbm,
    inv_hbm,
    lift_hbm,
    otr_hbm,
    clift_hbm,
    ctr_hbm,
    up_ref,
    cr_ref,
    next_ref,
    hess_ref,
    kry,
    inv,
    lift,
    otr,
    clift,
    ctr,
    gain_o,
    gain_c,
    off_o,
    off_c,
    outbuf,
    inbuf,
    faces,
    dbuf,
    parts,
    stats,
    load_sem,
    hop_sem,
    face_sem,
    stat_sem,
):
    S, C, Q = sizes
    total = S * C * Q
    s = lax.axis_index("stream")
    c = lax.axis_index("cross")
    q = lax.axis_index("pair")
    place = c * Q + q
    me = s * (C * Q) + place

    kry_copy = pltpu.make_async_copy(kry_hbm, kry, load_sem.at[0])
    kry_copy.start()
    groups = []
    for g in range(E // GROUP):
        span = pl.ds(g * GROUP, GROUP)
        copies = [
            pltpu.make_async_copy(src.at[span], dst.at[span], load_sem.at[2 + 4 * g + i])
            for i, (src, dst) in enumerate(
                ((inv_hbm, inv), (otr_hbm, otr), (ctr_hbm, ctr), (lift_hbm, lift))
            )
        ]
        for copy in copies:
            copy.start()
        groups.append(copies)
    clift_copy = pltpu.make_async_copy(clift_hbm, clift, load_sem.at[1])
    clift_copy.start()

    barrier = pltpu.get_barrier_semaphore()

    def others():
        for ds in range(S):
            for dc in range(C):
                for dq in range(Q):
                    if ds or dc or dq:
                        yield (lax.rem(s + ds, S), lax.rem(c + dc, C), lax.rem(q + dq, Q))

    for peer in others():
        pl.semaphore_signal(barrier, inc=1, device_id=peer, device_id_type=MESH)

    kry_copy.wait()
    for g in range(E // GROUP):
        for copy in groups[g]:
            copy.wait()
        for e in range(g * GROUP, (g + 1) * GROUP):
            cur = kry[KB - 1, :, e, :]
            hi = cur.astype(jnp.bfloat16).astype(jnp.float32)
            rows = jnp.concatenate(
                [hi, cur - hi, jnp.zeros((8, B), jnp.float32)], axis=0
            ).astype(jnp.bfloat16)
            left = jnp.concatenate([lift[e], rows], axis=0)
            for trace, gain, off in ((otr, gain_o, off_o), (ctr, gain_c, off_c)):
                t_hi, t_lo = split(dot(trace[e], inv[e]))
                out = dot_t(left, t_hi) + dot_t(left, t_lo)
                g_hi, g_lo = split(out[:R])
                gain[e, 0] = g_hi
                gain[e, 1] = g_lo
                off[e] = out[R : R + NV] + out[R + NV : R + 2 * NV]

    def gram():
        for n in range(NV):
            vs = [kry[k, n] for k in range(KB)]
            for i, (k, l) in enumerate(GRAM):
                row = NV * (KB + 1 + i) + n
                parts[row : row + 1, :] = lanes(vs[k] * vs[l])
        parts[NV * STATS :, :] = jnp.zeros((ROWS - NV * STATS, 128), jnp.float32)

    def lanes(x):
        x = jnp.sum(x, axis=0, keepdims=True)
        tail = jnp.concatenate([x[:, 256:B], jnp.zeros((1, 384 - B), jnp.float32)], axis=1)
        return x[:, :128] + x[:, 128:256] + tail

    pl.semaphore_wait(barrier, total - 1)

    hop = pltpu.make_async_remote_copy(
        src_ref=outbuf,
        dst_ref=inbuf,
        send_sem=hop_sem.at[0],
        recv_sem=hop_sem.at[1],
        device_id=(lax.rem(s + 1, S), c, q),
        device_id_type=MESH,
    )

    def face_copy(dc, dq):
        span = pl.ds(place * E, E)
        return pltpu.make_async_remote_copy(
            src_ref=faces.at[span],
            dst_ref=faces.at[span],
            send_sem=face_sem.at[0],
            recv_sem=face_sem.at[1],
            device_id=(s, lax.rem(c + dc, C), lax.rem(q + dq, Q)),
            device_id_type=MESH,
        )

    def send_faces():
        for dc in range(C):
            for dq in range(Q):
                if dc or dq:
                    face_copy(dc, dq).start()

    @pl.when(s == 0)
    def _():
        for e in range(E):
            outbuf[e] = off_o[e]
        if S > 1:
            hop.start()
        for e in range(E):
            faces[place * E + e] = off_c[e]
        send_faces()
        gram()

    @pl.when(s > 0)
    def _():
        gram()
        hop.wait_recv()

        @pl.when(s < S - 1)
        def _():
            for e in range(E):
                x = two_rows(inbuf[up_ref[0, e]])
                outbuf[e] = off_o[e] - fold(dot(x, gain_o[e, 0]) + dot(x, gain_o[e, 1]))
            hop.start()

        for e in range(E):
            x = two_rows(inbuf[up_ref[0, e]])
            faces[place * E + e] = off_c[e] - fold(dot(x, gain_c[e, 0]) + dot(x, gain_c[e, 1]))
        send_faces()

    clift_copy.wait()
    peers = C * Q - 1
    face_all = pltpu.make_async_remote_copy(
        src_ref=faces.at[pl.ds(0, peers * E)],
        dst_ref=faces.at[pl.ds(0, peers * E)],
        send_sem=face_sem.at[0],
        recv_sem=face_sem.at[1],
        device_id=(s, c, lax.rem(q + 1, Q)),
        device_id_type=MESH,
    )
    face_all.wait_recv()

    for e in range(E):
        x = two_rows(faces[cr_ref[0, e]])
        dbuf[:, e, :] = fold(dot(x, clift[e]))

    for n in range(NV):
        d = dbuf[n]
        for k in range(KB):
            parts[NV * k + n : NV * k + n + 1, :] = lanes(kry[k, n] * d)
        parts[NV * KB + n : NV * KB + n + 1, :] = lanes(d * d)

    diag = lax.broadcasted_iota(jnp.int32, (ROWS, 128), 0) == lax.broadcasted_iota(
        jnp.int32, (ROWS, 128), 1
    )
    column = jnp.sum(parts[...], axis=1, keepdims=True)
    stats[me] = jnp.sum(jnp.where(diag, column, 0.0), axis=0, keepdims=True)

    def stat_copy(peer):
        return pltpu.make_async_remote_copy(
            src_ref=stats.at[me],
            dst_ref=stats.at[me],
            send_sem=stat_sem.at[0],
            recv_sem=stat_sem.at[1],
            device_id=peer,
            device_id_type=MESH,
        )

    for peer in others():
        stat_copy(peer).start()
    stat_all = pltpu.make_async_remote_copy(
        src_ref=stats.at[pl.ds(0, total - 1)],
        dst_ref=stats.at[pl.ds(0, total - 1)],
        send_sem=stat_sem.at[0],
        recv_sem=stat_sem.at[1],
        device_id=(s, c, lax.rem(q + 1, Q)),
        device_id_type=MESH,
    )
    stat_all.wait_recv()

    row = jnp.sum(stats[...], axis=0)
    sums = jnp.sum(jnp.where(diag, row, 0.0), axis=1, keepdims=True)
    at = lambda i: sums[NV * i : NV * (i + 1)]
    dofs = float(E * B * total)
    entry = {}
    for i, (k, l) in enumerate(GRAM):
        entry[k, l] = entry[l, k] = at(KB + 1 + i)
    coeffs = [(entry[k, KB - 1] + at(k)) / dofs for k in range(KB)]
    rest = [(1.0 if k == KB - 1 else 0.0) - coeffs[k] for k in range(KB)]
    squares = at(KB)
    for k in range(KB):
        inner = 2.0 * at(k)
        for l in range(KB):
            inner += rest[l] * entry[k, l]
        squares += rest[k] * inner
    norm = jnp.sqrt(jnp.maximum(squares, 0.0) / dofs + 1e-06)
    scale = 1.0 / norm
    weights = [r * scale for r in rest]
    for n in range(NV):
        out = dbuf[n] * scale[n : n + 1]
        for k in range(KB):
            out += kry[k, n] * weights[k][n : n + 1]
        next_ref[n] = out
    hess_ref[...] = jnp.concatenate(coeffs + [norm], axis=1)
    face_all.wait_send()
    stat_all.wait_send()

    @pl.when(s < S - 1)
    def _():
        hop.wait_send()


def local(
    sizes,
    krylov_basis,
    inverse_blocks,
    inflow_lift,
    outflow_trace,
    cross_lift,
    cross_trace,
    upwind_element,
    cross_element,
):
    S, C, Q = sizes
    hbm = pl.BlockSpec(memory_space=pl.ANY)
    smem = pl.BlockSpec(memory_space=pltpu.SMEM)
    vmem = pl.BlockSpec(memory_space=pltpu.VMEM)
    bf16, f32 = jnp.bfloat16, jnp.float32
    next_vector, hessenberg = pl.pallas_call(
        functools.partial(kernel, sizes),
        out_shape=(
            jax.ShapeDtypeStruct((NV, E, B), f32),
            jax.ShapeDtypeStruct((NV, KB + 1), f32),
        ),
        in_specs=[hbm] * 6 + [smem] * 2,
        out_specs=(vmem, vmem),
        scratch_shapes=[
            pltpu.VMEM((KB, NV, E, B), f32),
            pltpu.VMEM((E, B, B), bf16),
            pltpu.VMEM((E, R, B), bf16),
            pltpu.VMEM((E, R, B), bf16),
            pltpu.VMEM((E, R, B), bf16),
            pltpu.VMEM((E, R, B), bf16),
            pltpu.VMEM((E, 2, R, R), bf16),
            pltpu.VMEM((E, 2, R, R), bf16),
            pltpu.VMEM((E, NV, R), f32),
            pltpu.VMEM((E, NV, R), f32),
            pltpu.VMEM((E, NV, R), f32),
            pltpu.VMEM((E, NV, R), f32),
            pltpu.VMEM((C * Q * E, NV, R), f32),
            pltpu.VMEM((NV, E, B), f32),
            pltpu.VMEM((ROWS, 128), f32),
            pltpu.VMEM((S * C * Q, 1, 128), f32),
            pltpu.SemaphoreType.DMA((2 + 4 * (E // GROUP),)),
            pltpu.SemaphoreType.DMA((2,)),
            pltpu.SemaphoreType.DMA((2,)),
            pltpu.SemaphoreType.DMA((2,)),
        ],
        compiler_params=pltpu.CompilerParams(collective_id=0, has_side_effects=True),
    )(
        krylov_basis[:, :, 0],
        inverse_blocks[0],
        jnp.swapaxes(inflow_lift[0], 1, 2),
        outflow_trace[0],
        jnp.swapaxes(cross_lift[0], 1, 2),
        cross_trace[0],
        upwind_element,
        cross_element,
    )
    return next_vector[:, None], hessenberg.T


def solution(mesh):
    sizes = tuple(mesh.shape[a] for a in ("stream", "cross", "pair"))
    return jax.shard_map(
        functools.partial(local, sizes),
        mesh=mesh,
        in_specs=(
            P(None, None, "stream", ("cross", "pair"), None),
            P("stream", ("cross", "pair"), None, None),
            P("stream", ("cross", "pair"), None, None),
            P("stream", ("cross", "pair"), None, None),
            P("stream", ("cross", "pair"), None, None),
            P("stream", ("cross", "pair"), None, None),
            P("stream", ("cross", "pair")),
            P("stream", ("cross", "pair")),
        ),
        out_specs=(P(None, "stream", ("cross", "pair"), None), P()),
        check_vma=False,
    )
```

time: 157 us -> 29.4 us (0.19)
  blocking collectives: 143 us -> 0 us
  Pallas kernels: 0 us -> 25.9 us
  matrix products: 9.66 us -> 0 us
    psum x2 -> x0, blocking collectives: 80.7 us -> none  [the longest x1 41.5 us: local(): lax.psum(jnp.sum(orthogonal * orthogonal, axis=(1, 2)), ('stream', 'cross...]
    all_gather x4 -> x0, blocking collectives: 62.3 us -> none  [the longest x3 53.1 us: carried_in(): gathered = jax.tree.map(lambda a: lax.all_gather(a, axis), part)]
    pallas_call x0 -> x1, Pallas kernels: none -> 25.9 us  [local(): pl.pallas_call(functools.partial(kernel, sizes), out_shape=(jax.ShapeDtyp...]
    dot_general x11 -> x0, matrix products: 9.66 us -> none  [the longest x1 1.73 us: local(): jnp.einsum('ebc,nec->neb', inverse_local, right_side, precision=highest)]
where the time goes in v1:
time: 29.4 us; the launch traced here: 29.2 us
  Pallas kernels  25.9 us (88%)
  local copies, waits for them, and re-layouts  2.66 us (9%)
  between operations  0.64 us (2%)
    pallas_call x1, Pallas kernels, local(): pl.pallas_call(functools.partial(kernel, sizes), out_shape=(jax.ShapeDtyp...  25.9 us
    unnamed x2, local copies, waits for them, and re-layouts  2.66 us

profile of v1, /device:TPU:0, one launch (start us, length us, event | category | flops | bytes accessed | tf_op | source)
XLA Modules:
  0.0 29.2 jit_solution(9411703167938461771)
XLA Ops:
  0.6 25.9 %shard_map.95 = (f32[4,8,320]{2,1,0:T(8,128)}, f32[4,5]{1,0:T(4,128)}) custom-call(f32[4,4,8,320]{3,2,1,0:T(8,128)} %bitcast.19, bf16[8,320,320]{2,1,0:T(8,128)(2,1)} %bitcast.14, bf16[8,80,320]{2,1,0:T(8,128)(2,1)} %bitcast.15, bf16[8,80,320]{2,1,0:T(8,128)(2,1)} %bitcast.16, bf16[8,80,320]{2,1,0:T(8,128)(2,1)} %bitcast.17, bf16[8,80,320]{2,1,0:T(8,128)(2,1)} %bitcast.18, ...), custom_call_target="tpu_custom_call" | custom-call | tf_op jit(solution)/shard_map/pallas_call | solution.py:300
  26.5 1.4 %copy.13 = f32[4,1,8,320]{3,2,1,0:T(8,128)} copy(f32[4,1,8,320]{3,2,1,0:T(8,128)} %bitcast.20) | data formatting | bytes 81920
  27.9 1.2 %copy.14 = f32[5,4]{0,1:T(4,128)} copy(f32[5,4]{0,1:T(4,128)} %bitcast.21) | data formatting | bytes 160

commit v2 on v1

--- a/solution.py
+++ b/solution.py
@@ -51,14 +51,15 @@
     ctr_hbm,
     up_ref,
     cr_ref,
-    next_ref,
-    hess_ref,
+    d_hbm,
+    row_ref,
     kry,
     inv,
     lift,
     otr,
     clift,
     ctr,
+    solved,
     gain_o,
     gain_c,
     off_o,
@@ -73,6 +74,8 @@
     hop_sem,
     face_sem,
     stat_sem,
+    out_sem,
+    back_sem,
 ):
     S, C, Q = sizes
     total = S * C * Q
@@ -82,23 +85,6 @@
     place = c * Q + q
     me = s * (C * Q) + place
 
-    kry_copy = pltpu.make_async_copy(kry_hbm, kry, load_sem.at[0])
-    kry_copy.start()
-    groups = []
-    for g in range(E // GROUP):
-        span = pl.ds(g * GROUP, GROUP)
-        copies = [
-            pltpu.make_async_copy(src.at[span], dst.at[span], load_sem.at[2 + 4 * g + i])
-            for i, (src, dst) in enumerate(
-                ((inv_hbm, inv), (otr_hbm, otr), (ctr_hbm, ctr), (lift_hbm, lift))
-            )
-        ]
-        for copy in copies:
-            copy.start()
-        groups.append(copies)
-    clift_copy = pltpu.make_async_copy(clift_hbm, clift, load_sem.at[1])
-    clift_copy.start()
-
     barrier = pltpu.get_barrier_semaphore()
 
     def others():
@@ -108,27 +94,85 @@
                     if ds or dc or dq:
                         yield (lax.rem(s + ds, S), lax.rem(c + dc, C), lax.rem(q + dq, Q))
 
-    for peer in others():
-        pl.semaphore_signal(barrier, inc=1, device_id=peer, device_id_type=MESH)
+    for dc in range(C):
+        for dq in range(Q):
+            if dc or dq:
+                pl.semaphore_signal(
+                    barrier,
+                    inc=1,
+                    device_id=(s, lax.rem(c + dc, C), lax.rem(q + dq, Q)),
+                    device_id_type=MESH,
+                )
+    for edge, step in ((S - 1, 1), (0, S - 1)):
+
+        @pl.when(s != edge)
+        def _():
+            pl.semaphore_signal(
+                barrier, inc=1, device_id=(lax.rem(s + step, S), c, q), device_id_type=MESH
+            )
+
+    kry_copy = pltpu.make_async_copy(kry_hbm, kry, load_sem.at[0])
+    inv_copies = [
+        pltpu.make_async_copy(
+            inv_hbm.at[pl.ds(g * GROUP, GROUP)], inv.at[pl.ds(g * GROUP, GROUP)], load_sem.at[5 + g]
+        )
+        for g in range(E // GROUP)
+    ]
+    otr_copy = pltpu.make_async_copy(otr_hbm, otr, load_sem.at[1])
+    lift_copy = pltpu.make_async_copy(lift_hbm, lift, load_sem.at[2])
+    ctr_copy = pltpu.make_async_copy(ctr_hbm, ctr, load_sem.at[3])
+    clift_copy = pltpu.make_async_copy(clift_hbm, clift, load_sem.at[4])
+    for copy in [kry_copy, lift_copy] + inv_copies + [otr_copy, ctr_copy, clift_copy]:
+        copy.start()
+
+    def current_rows(e):
+        cur = kry[KB - 1, :, e, :]
+        hi = cur.astype(jnp.bfloat16).astype(jnp.float32)
+        return jnp.concatenate(
+            [hi, cur - hi, jnp.zeros((8, B), jnp.float32)], axis=0
+        ).astype(jnp.bfloat16)
+
+    def offsets(trace, off):
+        for e in range(E):
+            off[e] = fold(dot_t(solved[e, 0, R : R + 2 * NV], trace[e]))
+
+    def gains(trace, gain, off):
+        for e in range(E):
+            out = dot_t(solved[e, 0], trace[e]) + dot_t(solved[e, 1], trace[e])
+            g_hi, g_lo = split(out[:R])
+            gain[e, 0] = g_hi
+            gain[e, 1] = g_lo
+            off[e] = out[R : R + NV] + out[R + NV : R + 2 * NV]
 
     kry_copy.wait()
-    for g in range(E // GROUP):
-        for copy in groups[g]:
-            copy.wait()
-        for e in range(g * GROUP, (g + 1) * GROUP):
-            cur = kry[KB - 1, :, e, :]
-            hi = cur.astype(jnp.bfloat16).astype(jnp.float32)
-            rows = jnp.concatenate(
-                [hi, cur - hi, jnp.zeros((8, B), jnp.float32)], axis=0
-            ).astype(jnp.bfloat16)
-            left = jnp.concatenate([lift[e], rows], axis=0)
-            for trace, gain, off in ((otr, gain_o, off_o), (ctr, gain_c, off_c)):
-                t_hi, t_lo = split(dot(trace[e], inv[e]))
-                out = dot_t(left, t_hi) + dot_t(left, t_lo)
-                g_hi, g_lo = split(out[:R])
-                gain[e, 0] = g_hi
-                gain[e, 1] = g_lo
-                off[e] = out[R : R + NV] + out[R + NV : R + 2 * NV]
+    lift_copy.wait()
+
+    @pl.when(s == 0)
+    def _():
+        for e in range(E):
+            if e % GROUP == 0:
+                inv_copies[e // GROUP].wait()
+            y = two_rows(fold(dot_t(current_rows(e), inv[e])[: 2 * NV]))
+            solved[e, 0, R : R + 2 * NV] = y
+        otr_copy.wait()
+        offsets(otr, off_o)
+
+    @pl.when(s > 0)
+    def _():
+        for e in range(E):
+            if e % GROUP == 0:
+                inv_copies[e // GROUP].wait()
+            left = jnp.concatenate([lift[e], current_rows(e)], axis=0)
+            hi, lo = split(dot_t(left, inv[e]))
+            solved[e, 0] = hi
+            solved[e, 1] = lo
+        otr_copy.wait()
+
+    @pl.when(lax.rem(s, S - 1) > 0)
+    def _():
+        gains(otr, gain_o, off_o)
+
+    ctr_copy.wait()
 
     def gram():
         for n in range(NV):
@@ -143,7 +187,13 @@
         tail = jnp.concatenate([x[:, 256:B], jnp.zeros((1, 384 - B), jnp.float32)], axis=1)
         return x[:, :128] + x[:, 128:256] + tail
 
-    pl.semaphore_wait(barrier, total - 1)
+    @pl.when(lax.rem(s, S - 1) == 0)
+    def _():
+        pl.semaphore_wait(barrier, C * Q)
+
+    @pl.when(lax.rem(s, S - 1) > 0)
+    def _():
+        pl.semaphore_wait(barrier, C * Q + 1)
 
     hop = pltpu.make_async_remote_copy(
         src_ref=outbuf,
@@ -175,8 +225,8 @@
     def _():
         for e in range(E):
             outbuf[e] = off_o[e]
-        if S > 1:
-            hop.start()
+        hop.start()
+        offsets(ctr, off_c)
         for e in range(E):
             faces[place * E + e] = off_c[e]
         send_faces()
@@ -184,7 +234,11 @@
 
     @pl.when(s > 0)
     def _():
-        gram()
+        @pl.when(s > 1)
+        def _():
+            gains(ctr, gain_c, off_c)
+            gram()
+
         hop.wait_recv()
 
         @pl.when(s < S - 1)
@@ -194,10 +248,26 @@
                 outbuf[e] = off_o[e] - fold(dot(x, gain_o[e, 0]) + dot(x, gain_o[e, 1]))
             hop.start()
 
+        @pl.when(s == 1)
+        def _():
+            gains(ctr, gain_c, off_c)
+
         for e in range(E):
             x = two_rows(inbuf[up_ref[0, e]])
             faces[place * E + e] = off_c[e] - fold(dot(x, gain_c[e, 0]) + dot(x, gain_c[e, 1]))
         send_faces()
+
+        @pl.when(s == 1)
+        def _():
+            gram()
+
+    @pl.when(s < S - 1)
+    def _():
+        pl.semaphore_wait(back_sem, 1)
+
+    @pl.when(s > 0)
+    def _():
+        pl.semaphore_signal(back_sem, inc=1, device_id=(s - 1, c, q), device_id_type=MESH)
 
     clift_copy.wait()
     peers = C * Q - 1
@@ -215,6 +285,8 @@
         x = two_rows(faces[cr_ref[0, e]])
         dbuf[:, e, :] = fold(dot(x, clift[e]))
 
+    d_copy = pltpu.make_async_copy(dbuf, d_hbm, out_sem)
+    d_copy.start()
     for n in range(NV):
         d = dbuf[n]
         for k in range(KB):
@@ -249,10 +321,22 @@
     )
     stat_all.wait_recv()
 
-    row = jnp.sum(stats[...], axis=0)
-    sums = jnp.sum(jnp.where(diag, row, 0.0), axis=1, keepdims=True)
+    row_ref[...] = jnp.sum(stats[...], axis=0)
+    d_copy.wait()
+    face_all.wait_send()
+    stat_all.wait_send()
+
+    @pl.when(s < S - 1)
+    def _():
+        hop.wait_send()
+
+
+def finish(dofs, d_ref, row_ref, kry, next_ref, hess_ref):
+    diag = lax.broadcasted_iota(jnp.int32, (ROWS, 128), 0) == lax.broadcasted_iota(
+        jnp.int32, (ROWS, 128), 1
+    )
+    sums = jnp.sum(jnp.where(diag, row_ref[...], 0.0), axis=1, keepdims=True)
     at = lambda i: sums[NV * i : NV * (i + 1)]
-    dofs = float(E * B * total)
     entry = {}
     for i, (k, l) in enumerate(GRAM):
         entry[k, l] = entry[l, k] = at(KB + 1 + i)
@@ -268,17 +352,11 @@
     scale = 1.0 / norm
     weights = [r * scale for r in rest]
     for n in range(NV):
-        out = dbuf[n] * scale[n : n + 1]
+        out = d_ref[n] * scale[n : n + 1]
         for k in range(KB):
             out += kry[k, n] * weights[k][n : n + 1]
         next_ref[n] = out
     hess_ref[...] = jnp.concatenate(coeffs + [norm], axis=1)
-    face_all.wait_send()
-    stat_all.wait_send()
-
-    @pl.when(s < S - 1)
-    def _():
-        hop.wait_send()
 
 
 def local(
@@ -297,14 +375,15 @@
     smem = pl.BlockSpec(memory_space=pltpu.SMEM)
     vmem = pl.BlockSpec(memory_space=pltpu.VMEM)
     bf16, f32 = jnp.bfloat16, jnp.float32
-    next_vector, hessenberg = pl.pallas_call(
+    basis = krylov_basis[:, :, 0]
+    image, sums = pl.pallas_call(
         functools.partial(kernel, sizes),
         out_shape=(
             jax.ShapeDtypeStruct((NV, E, B), f32),
-            jax.ShapeDtypeStruct((NV, KB + 1), f32),
+            jax.ShapeDtypeStruct((1, 128), f32),
         ),
         in_specs=[hbm] * 6 + [smem] * 2,
-        out_specs=(vmem, vmem),
+        out_specs=(hbm, vmem),
         scratch_shapes=[
             pltpu.VMEM((KB, NV, E, B), f32),
             pltpu.VMEM((E, B, B), bf16),
@@ -312,6 +391,7 @@
             pltpu.VMEM((E, R, B), bf16),
             pltpu.VMEM((E, R, B), bf16),
             pltpu.VMEM((E, R, B), bf16),
+            pltpu.VMEM((E, 2, R + 16, B), bf16),
             pltpu.VMEM((E, 2, R, R), bf16),
             pltpu.VMEM((E, 2, R, R), bf16),
             pltpu.VMEM((E, NV, R), f32),
@@ -322,14 +402,16 @@
             pltpu.VMEM((NV, E, B), f32),
             pltpu.VMEM((ROWS, 128), f32),
             pltpu.VMEM((S * C * Q, 1, 128), f32),
-            pltpu.SemaphoreType.DMA((2 + 4 * (E // GROUP),)),
+            pltpu.SemaphoreType.DMA((5 + E // GROUP,)),
             pltpu.SemaphoreType.DMA((2,)),
             pltpu.SemaphoreType.DMA((2,)),
             pltpu.SemaphoreType.DMA((2,)),
+            pltpu.SemaphoreType.DMA,
+            pltpu.SemaphoreType.REGULAR,
         ],
         compiler_params=pltpu.CompilerParams(collective_id=0, has_side_effects=True),
     )(
-        krylov_basis[:, :, 0],
+        basis,
         inverse_blocks[0],
         jnp.swapaxes(inflow_lift[0], 1, 2),
         outflow_trace[0],
@@ -338,6 +420,15 @@
         upwind_element,
         cross_element,
     )
+    next_vector, hessenberg = pl.pallas_call(
+        functools.partial(finish, float(E * B * S * C * Q)),
+        out_shape=(
+            jax.ShapeDtypeStruct((NV, E, B), f32),
+            jax.ShapeDtypeStruct((NV, KB + 1), f32),
+        ),
+        in_specs=[vmem] * 3,
+        out_specs=(vmem, vmem),
+    )(image, sums, basis)
     return next_vector[:, None], hessenberg.T
 
 

time: 29.4 us -> 25.3 us (0.86)
  local copies, waits for them, and re-layouts: 2.66 us -> 0 us
  Pallas kernels: 25.9 us -> 24.5 us
    pallas_call x1, Pallas kernels: 25.9 us -> 22.8 us  [local(): pl.pallas_call(functools.partial(kernel, sizes), out_shape=(jax.ShapeDtyp...]
    unnamed x2 -> x0, local copies, waits for them, and re-layouts: 2.66 us -> none
    pallas_call x0 -> x1, Pallas kernels: none -> 1.75 us  [local(): pl.pallas_call(functools.partial(finish, float(E * B * S * C * Q)), out_s...]
where the time goes in v2:
time: 25.3 us; the launch traced here: 25.1 us
  Pallas kernels  24.5 us (97%)
  between operations  0.64 us (3%)
    pallas_call x1, Pallas kernels, local(): pl.pallas_call(functools.partial(kernel, sizes), out_shape=(jax.ShapeDtyp...  22.8 us
    pallas_call x1, Pallas kernels, local(): pl.pallas_call(functools.partial(finish, float(E * B * S * C * Q)), out_s...  1.75 us

profile of v2, /device:TPU:0, one launch (start us, length us, event | category | flops | bytes accessed | tf_op | source)
XLA Modules:
  0.0 25.1 jit_solution(15236351454927267190)
XLA Ops:
  0.6 22.8 %shard_map.95 = (f32[4,8,320]{2,1,0:T(8,128)}, f32[1,128]{1,0:T(1,128)}) custom-call(f32[4,4,8,320]{3,2,1,0:T(8,128)} %bitcast.15, bf16[8,320,320]{2,1,0:T(8,128)(2,1)} %bitcast.14, bf16[8,80,320]{2,1,0:T(8,128)(2,1)} %bitcast.17, bf16[8,80,320]{2,1,0:T(8,128)(2,1)} %bitcast.18, bf16[8,80,320]{2,1,0:T(8,128)(2,1)} %bitcast.19, bf16[8,80,320]{2,1,0:T(8,128)(2,1)} %bitcast.20, ...), custom_call_target="tpu_custom_call" | custom-call | tf_op jit(solution)/shard_map/pallas_call | solution.py:379
  23.4 1.8 %shard_map.96 = (f32[4,8,320]{2,1,0:T(8,128)}, f32[4,5]{1,0:T(4,128)}) custom-call(f32[4,8,320]{2,1,0:T(8,128)} %get-tuple-element.6.d_ref, f32[1,128]{1,0:T(1,128)} %get-tuple-element.7.row_ref, f32[4,4,8,320]{3,2,1,0:T(8,128)} %bitcast.16), custom_call_target="tpu_custom_call" | custom-call | tf_op jit(solution)/shard_map/pallas_call | solution.py:423

commit v3 on v2

--- a/solution.py
+++ b/solution.py
@@ -88,9 +88,9 @@
     barrier = pltpu.get_barrier_semaphore()
 
     def others():
-        for ds in range(S):
-            for dc in range(C):
-                for dq in range(Q):
+        for ds in [*range(1, S), 0]:
+            for dc in [*range(1, C), 0]:
+                for dq in [*range(1, Q), 0]:
                     if ds or dc or dq:
                         yield (lax.rem(s + ds, S), lax.rem(c + dc, C), lax.rem(q + dq, Q))
 
@@ -111,7 +111,9 @@
                 barrier, inc=1, device_id=(lax.rem(s + step, S), c, q), device_id_type=MESH
             )
 
-    kry_copy = pltpu.make_async_copy(kry_hbm, kry, load_sem.at[0])
+    last, rest = pl.ds(KB - 1, 1), pl.ds(0, KB - 1)
+    current_copy = pltpu.make_async_copy(kry_hbm.at[last], kry.at[last], load_sem.at[0])
+    kry_copy = pltpu.make_async_copy(kry_hbm.at[rest], kry.at[rest], load_sem.at[5 + E // GROUP])
     inv_copies = [
         pltpu.make_async_copy(
             inv_hbm.at[pl.ds(g * GROUP, GROUP)], inv.at[pl.ds(g * GROUP, GROUP)], load_sem.at[5 + g]
@@ -122,8 +124,20 @@
     lift_copy = pltpu.make_async_copy(lift_hbm, lift, load_sem.at[2])
     ctr_copy = pltpu.make_async_copy(ctr_hbm, ctr, load_sem.at[3])
     clift_copy = pltpu.make_async_copy(clift_hbm, clift, load_sem.at[4])
-    for copy in [kry_copy, lift_copy] + inv_copies + [otr_copy, ctr_copy, clift_copy]:
-        copy.start()
+    current_copy.start()
+
+    @pl.when(s == 0)
+    def _():
+        for copy in inv_copies + [otr_copy, ctr_copy, lift_copy]:
+            copy.start()
+
+    @pl.when(s > 0)
+    def _():
+        for copy in [lift_copy] + inv_copies + [otr_copy, ctr_copy]:
+            copy.start()
+
+    kry_copy.start()
+    clift_copy.start()
 
     def current_rows(e):
         cur = kry[KB - 1, :, e, :]
@@ -144,8 +158,7 @@
             gain[e, 1] = g_lo
             off[e] = out[R : R + NV] + out[R + NV : R + 2 * NV]
 
-    kry_copy.wait()
-    lift_copy.wait()
+    current_copy.wait()
 
     @pl.when(s == 0)
     def _():
@@ -159,6 +172,7 @@
 
     @pl.when(s > 0)
     def _():
+        lift_copy.wait()
         for e in range(E):
             if e % GROUP == 0:
                 inv_copies[e // GROUP].wait()
@@ -171,8 +185,6 @@
     @pl.when(lax.rem(s, S - 1) > 0)
     def _():
         gains(otr, gain_o, off_o)
-
-    ctr_copy.wait()
 
     def gram():
         for n in range(NV):
@@ -226,14 +238,20 @@
         for e in range(E):
             outbuf[e] = off_o[e]
         hop.start()
+        ctr_copy.wait()
         offsets(ctr, off_c)
         for e in range(E):
             faces[place * E + e] = off_c[e]
         send_faces()
+        lift_copy.wait()
+        kry_copy.wait()
         gram()
 
     @pl.when(s > 0)
     def _():
+        ctr_copy.wait()
+        kry_copy.wait()
+
         @pl.when(s > 1)
         def _():
             gains(ctr, gain_c, off_c)
@@ -402,7 +420,7 @@
             pltpu.VMEM((NV, E, B), f32),
             pltpu.VMEM((ROWS, 128), f32),
             pltpu.VMEM((S * C * Q, 1, 128), f32),
-            pltpu.SemaphoreType.DMA((5 + E // GROUP,)),
+            pltpu.SemaphoreType.DMA((6 + E // GROUP,)),
             pltpu.SemaphoreType.DMA((2,)),
             pltpu.SemaphoreType.DMA((2,)),
             pltpu.SemaphoreType.DMA((2,)),

time: 25.3 us -> 25.1 us (level)
  no operation moved by 1% of the time
where the time goes in v3:
time: 25.1 us; the launch traced here: 24.9 us
  Pallas kernels  24.3 us (97%)
  between operations  0.64 us (3%)
    pallas_call x1, Pallas kernels, local(): pl.pallas_call(functools.partial(kernel, sizes), out_shape=(jax.ShapeDtyp...  22.5 us
    pallas_call x1, Pallas kernels, local(): pl.pallas_call(functools.partial(finish, float(E * B * S * C * Q)), out_s...  1.75 us

profile of v3, /device:TPU:0, one launch (start us, length us, event | category | flops | bytes accessed | tf_op | source)
XLA Modules:
  0.0 24.9 jit_solution(11907252390425513665)
XLA Ops:
  0.6 22.5 %shard_map.95 = (f32[4,8,320]{2,1,0:T(8,128)}, f32[1,128]{1,0:T(1,128)}) custom-call(f32[4,4,8,320]{3,2,1,0:T(8,128)} %bitcast.15, bf16[8,320,320]{2,1,0:T(8,128)(2,1)} %bitcast.14, bf16[8,80,320]{2,1,0:T(8,128)(2,1)} %bitcast.17, bf16[8,80,320]{2,1,0:T(8,128)(2,1)} %bitcast.18, bf16[8,80,320]{2,1,0:T(8,128)(2,1)} %bitcast.19, bf16[8,80,320]{2,1,0:T(8,128)(2,1)} %bitcast.20, ...), custom_call_target="tpu_custom_call" | custom-call | tf_op jit(solution)/shard_map/pallas_call | solution.py:397
  23.2 1.8 %shard_map.96 = (f32[4,8,320]{2,1,0:T(8,128)}, f32[4,5]{1,0:T(4,128)}) custom-call(f32[4,8,320]{2,1,0:T(8,128)} %get-tuple-element.6.d_ref, f32[1,128]{1,0:T(1,128)} %get-tuple-element.7.row_ref, f32[4,4,8,320]{3,2,1,0:T(8,128)} %bitcast.16), custom_call_target="tpu_custom_call" | custom-call | tf_op jit(solution)/shard_map/pallas_call | solution.py:441
